TPU v7x, 32 devices: a whole 2x2x4 slice. The times are simulated.
32 devices in a mesh: groups: 2 (over y), cell: 4 (over z), wall: 4 (over x, core).
Axes of the slice: x: 2, y: 2, z: 4, core: 2. Of those that a mesh axis runs over, the one named last changes fastest.
Arguments:
- mem_pos: float32 [3, 2048], P(None, ('groups', 'cell')), parts along dimension 1, may hold values from -0.7 to 8, as said below
- forces: bfloat16 [32, 3, 2048], P(None, None, ('groups', 'cell', 'wall')), parts along dimension 2, may hold values from -1.59375 to 1.59375
- wall_pos: float32 [3, 1024], P(None, ('groups', 'wall')), parts along dimension 1, may hold values from -1 to 8, as said below
- wall_normal: float32 [3, 1024], P(None, ('groups', 'wall')), parts along dimension 1, as said below
- wall_data: float32 [32, 3, 1024], P(None, None, ('groups', 'wall')), parts along dimension 2, may hold values from -6 to 6
- lag_density: bfloat16 [16, 3, 1024], P(None, None, ('groups', 'wall', 'cell')), parts along dimension 2, may hold values from -15 to 15
- batch_order: int32 [32], replicated, may hold values from 0 to 31, each once
Outputs:
- membrane_velocity: float32 [32, 3, 2048], P(None, None, ('groups', 'cell', 'wall')), parts along dimension 2
- wall_density: float32 [16, 3, 1024], P(None, None, ('groups', 'wall', 'cell')), parts along dimension 2
There are 2 independent parts, one for each index of `groups`. A program takes and returns all parts, laid end to end along the dimension named above; an argument that names none is the same for every part. Nothing has to cross between parts.
Inputs may be any that keep to these rules, and one draw needn't show every extreme that they name: `mem_pos`: each membrane point lies within 0.7 of the vessel axis (first two coordinates) with third coordinate between 0 and 8. `wall_pos`: each wall point lies on the unit cylinder around the vessel axis, third coordinate between 0 and 8. `wall_normal`: column w is the outward unit normal of the cylinder at wall_pos[:, w] times 16 pi / 512.
All inputs are finite; a program needn't handle non-finite values.
Results may differ from a plain program's by a relative error of at most 0.002.
Values may be sent and summed in bfloat16 or wider, within the bound.
A program may use at most 64 MiB of HBM per device.

v0:
```python
import math

import jax
import jax.numpy as jnp
from jax import lax
from jax.sharding import PartitionSpec as P

stokes_coef = 1.0 / (8.0 * math.pi)


def single_tile(targets, sources):
    separation = targets[:, None, :] - sources[:, :, None]
    inverse = lax.rsqrt(jnp.sum(separation * separation, axis=0))
    inverse_cube = inverse * inverse * inverse
    stacked = []
    for second_dim in range(3):
        entries_row = []
        for first_dim in range(3):
            element = separation[first_dim] * separation[second_dim] * inverse_cube
            if first_dim == second_dim:
                element = element + inverse
            entries_row.append(element * stokes_coef)
        stacked.append(jnp.stack(entries_row, axis=1))
    kernel_tile = jnp.stack(stacked, axis=0)
    return kernel_tile.reshape(3 * sources.shape[1], 3 * targets.shape[1]).astype(jnp.bfloat16)


def double_tile(targets, sources, normals):
    separation = targets[:, None, :] - sources[:, :, None]
    inverse = lax.rsqrt(jnp.sum(separation * separation, axis=0))
    normal_flux = jnp.sum(separation * normals[:, :, None], axis=0)
    weight = -6.0 * stokes_coef * normal_flux * inverse**5
    stacked = []
    for second_dim in range(3):
        entries_row = []
        for first_dim in range(3):
            entries_row.append(weight * separation[first_dim] * separation[second_dim])
        stacked.append(jnp.stack(entries_row, axis=1))
    kernel_tile = jnp.stack(stacked, axis=0)
    return kernel_tile.reshape(3 * sources.shape[1], 3 * targets.shape[1]).astype(jnp.bfloat16)


def shards(mem_pos, forces, wall_pos, wall_normal, wall_data, lag_density, batch_order):
    columns = forces.shape[0]
    halfway = columns // 2
    point_count = mem_pos.shape[1]
    wall_count = wall_pos.shape[1]
    shard_width = lag_density.shape[2]
    piece_len = math.gcd(point_count, 128)
    block_count = point_count // piece_len
    first_rows = batch_order[:halfway]
    second_rows = batch_order[halfway:]
    force_block = lax.all_gather(forces, "wall", axis=2, tiled=True)
    lag_block = lax.all_gather(lag_density, "cell", axis=2, tiled=True)
    lag_flat = lag_block.reshape(halfway, 3 * wall_count)

    def position_at(block_index):
        return lax.dynamic_slice_in_dim(mem_pos, block_index * piece_len, piece_len, 1)

    def single_term(block_index):
        loaded = lax.dynamic_slice_in_dim(force_block, block_index * piece_len, piece_len, 2)
        loaded = loaded.reshape(columns, 3 * piece_len)
        return jnp.dot(
            loaded,
            single_tile(wall_pos, position_at(block_index)),
            preferred_element_type=jnp.float32,
        )

    def double_term(dense_rows, block_index):
        kernel_tile = double_tile(position_at(block_index), wall_pos, wall_normal)
        product = jnp.dot(dense_rows, kernel_tile, preferred_element_type=jnp.float32)
        return product.reshape(dense_rows.shape[0], 3, piece_len)

    def place_block(target, piece, block_index):
        return lax.dynamic_update_slice_in_dim(target, piece, block_index * piece_len, 2)

    empty_wall = jnp.zeros((columns, 3 * wall_count), jnp.float32)

    def add_single(block_index, running):
        return running + single_term(block_index)

    running = lax.fori_loop(0, block_count, add_single, empty_wall)
    wall_term = running.reshape(columns, 3, wall_count)
    position_cell = lax.axis_index("cell")
    first_sum = lax.psum(jnp.take(wall_term, first_rows, axis=0), "cell")
    first_block = (2.0 * (jnp.take(wall_data, first_rows, axis=0) - first_sum)).astype(jnp.bfloat16)
    second_sum = lax.psum_scatter(
        jnp.take(wall_term, second_rows, axis=0).astype(jnp.bfloat16),
        "cell",
        scatter_dimension=2,
        tiled=True,
    ).astype(jnp.float32)
    second_data = lax.dynamic_slice_in_dim(
        jnp.take(wall_data, second_rows, axis=0), position_cell * shard_width, shard_width, 2
    )
    wall_density = 2.0 * (second_data - second_sum)
    first_flat = first_block.reshape(halfway, 3 * wall_count)
    carried = jnp.concatenate([lag_flat, first_flat], axis=0)

    def all_terms(block_index, target):
        return place_block(target, double_term(carried, block_index), block_index)

    membrane_term = lax.fori_loop(
        0, block_count, all_terms, jnp.zeros((columns, 3, point_count), jnp.float32)
    )
    batched = lax.psum_scatter(membrane_term, "wall", scatter_dimension=2, tiled=True)
    membrane_velocity = jnp.zeros_like(batched).at[batch_order].set(batched)
    return (membrane_velocity, wall_density)


def solution(mesh):
    placed = (
        P(None, ("groups", "cell")),
        P(None, None, ("groups", "cell", "wall")),
        P(None, ("groups", "wall")),
        P(None, ("groups", "wall")),
        P(None, None, ("groups", "wall")),
        P(None, None, ("groups", "wall", "cell")),
        P(),
    )
    return jax.shard_map(
        shards,
        mesh=mesh,
        in_specs=placed,
        out_specs=(
            P(None, None, ("groups", "cell", "wall")),
            P(None, None, ("groups", "wall", "cell")),
        ),
        check_vma=False,
    )
```

profile of v0, /device:TPU:0, one launch (start us, length us, event | category | flops | bytes accessed | tf_op | source)
XLA Modules:
  0.0 100.6 jit_solution(6531965876027255350)
XLA Ops:
  7.2 0.8 compare_and_fusion
  8.1 0.8 copy.57
  8.9 7.2 %all_gather.7 = bf16[32,3,256]{0,1,2:T(4,128)(2,1)S(1)} all-gather(bf16[32,3,64]{0,1,2:T(4,128)(2,1)S(1)} %copy.57), channel_id=1, replica_groups=mesh['groups'=2,'cell'=4,'wall'=4] {'wall'}, dimensions={2}, use_global_device_ids=true | all-gather | bytes 61440 | tf_op jit(solution)/shard_map/all_gather | solution.py:53
  16.3 4.3 %while.28 = (s32[]{:T(128)}, f32[32,384]{1,0:T(8,128)S(1)}, bf16[32,3,256]{2,1,0:T(4,128)(2,1)S(1)}, f32[3,128]{1,0:T(4,128)}, f32[3,256]{1,0:T(4,128)}, /*index=5*/s32[]{:T(128)}, s32[]{:T(128)}, s32[]{:T(128)}, s32[]{:T(128)}) while((s32[]{:T(128)}, f32[32,384]{1,0:T(8,128)S(1)}, bf16[32,3,256]{2,1,0:T(4,128)(2,1)S(1)}, ...), condition=%wide.region_2.4_spmd.clone, body=%wide.region_0.3_spmd.clone.sunk | while | flops 10657799 | bytes 2865309 | solution.py:82
  16.3 0.7 constant_dynamic-slice_fusion.7
  17.0 0.8 multiply_reduce_fusion.6
  18.5 0.7 constant_dynamic-slice_fusion.7
  19.2 0.8 multiply_reduce_fusion.6
  21.5 0.7 reshape.610
  23.0 19.2 %psum.7 = f32[16,3,128]{2,0,1:T(8,128)S(1)} all-reduce(f32[16,3,128]{2,0,1:T(8,128)S(1)} %copy_select_fusion.1), channel_id=1, replica_groups=mesh['groups'=2,'cell'=4,'wall'=4] {'cell'}, use_global_device_ids=true, to_apply=%region_3.0 | all-reduce | flops 6144 | bytes 49152 | tf_op jit(solution)/shard_map/psum | solution.py:85
  42.9 13.4 %all_gather.6 = bf16[16,3,128]{0,1,2:T(4,128)(2,1)S(1)} all-gather(bf16[16,3,32]{0,1,2:T(4,128)(2,1)S(1)} %copy.55), channel_id=1, replica_groups=mesh['groups'=2,'cell'=4,'wall'=4] {'cell'}, dimensions={2}, use_global_device_ids=true | all-gather | bytes 15360 | tf_op jit(solution)/shard_map/all_gather | solution.py:54
  56.5 4.5 %while.27 = (s32[]{:T(128)}, f32[32,3,256]{2,1,0:T(4,128)S(1)}, f32[3,256]{1,0:T(4,128)}, f32[3,128]{1,0:T(4,128)}, f32[3,128]{1,0:T(4,128)S(1)}, /*index=5*/bf1...) while((s32[]{:T(128)}, f32[32,3,256]{2,1,0:T(4,128)S(1)}, f32[3,256]{1,0:T(4,128)}, ...), condition=%wide.region_7.0_spmd, body=%wide.region_4.8_spmd.sunk | while | flops 10682374 | bytes 3522203 | solution.py:103
  56.6 0.7 constant_dynamic-slice_fusion.6
  57.2 0.9 multiply_reduce_fusion.5
  58.8 0.7 constant_dynamic-slice_fusion.6
  59.5 0.9 multiply_reduce_fusion.5
  61.1 4.4 %copy.63 = f32[32,3,256]{1,0,2:T(8,128)} copy(f32[32,3,256]{2,1,0:T(4,128)S(1)} %get-tuple-element.207) | data formatting | bytes 196608
  65.5 5.5 %reshape.608 = f32[256,96]{1,0:T(8,128)} reshape(f32[256,32,3]{2,1,0:T(8,128)} %bitcast.197) | data formatting | bytes 196608
  71.7 0.8 reshape.611
  72.5 0.7 fusion.27
  73.2 15.8 %reduce-scatter.7.cloned.1.call-done = f32[64,96]{1,0:T(8,128)} async-done(((f32[256,96]{1,0:T(8,128)}), f32[64,96]{1,0:T(8,128)}) %reduce-scatter.7.cloned.1.call-update) | async-done | bytes 24592
  89.0 1.8 %reshape.609 = f32[64,32,3]{2,1,0:T(8,128)S(1)} reshape(f32[64,96]{1,0:T(8,128)} %reduce-scatter.7.cloned.1.call-done) | data formatting | bytes 49152
  90.9 0.7 copy.64
  91.6 1.5 %scatter_fusion = f32[32,3,64]{2,1,0:T(4,128)S(1)} fusion(f32[32,3,64]{2,1,0:T(4,128)S(1)} %broadcast_in_dim.36, s32[32]{0:T(128)S(1)} %compare_select_fusion.2, f32[32,3,64]{2,1,0:T(4,128)S(1)} %copy.64), kind=kCustom, calls=%fused_computation.4 | custom fusion | bytes 73856 | tf_op jit(solution)/shard_map/scatter | solution.py:107
  (65 shorter events, 6.5 us)
Async XLA Ops:
  7.2 35.0 %copy-start = (f32[32,3,128]{2,0,1:T(8,128)S(1)}, f32[32,3,128]{2,0,1:T(8,128)}, u32[]{:S(2)}) copy-start(f32[32,3,128]{2,0,1:T(8,128)} %param.17) | copy-start | bytes 147460
  7.2 64.5 %reduce-scatter.9.cloned.1.call-start = ((), (), s32[]{:S(2)}) async-start(), calls=%async_computation.3 | async-start | bytes 40960
  16.3 26.5 %copy-start.2 = (bf16[16,3,32]{2,0,1:T(8,128)(2,1)S(1)}, bf16[16,3,32]{2,0,1:T(8,128)(2,1)}, u32[]{:S(2)}) copy-start(bf16[16,3,32]{2,0,1:T(8,128)(2,1)} %param.18) | copy-start | bytes 9220
  16.3 40.2 %copy-start.1 = (f32[3,128]{1,0:T(4,128)S(1)}, f32[3,128]{1,0:T(4,128)}, u32[]{:S(2)}) copy-start(f32[3,128]{1,0:T(4,128)} %param.16) | copy-start | bytes 4612
  22.2 66.8 %reduce-scatter.7.cloned.1.call-start = ((), (), s32[]{:S(2)}) async-start(), calls=%async_computation.2 | async-start | bytes 163840
  61.1 10.5 %copy-start.3 = (s32[32]{0:T(128)S(1)}, s32[32]{0:T(128)}, u32[]{:S(2)}) copy-start(s32[32]{0:T(128)} %param.19) | copy-start | bytes 388
Sparse Core Ops, SparseCore 0:
  22.3 20.5 reduce-scatter.8
  71.1 17.8 reduce-scatter.6
where the time goes:
time: 101 us
  blocking collectives  39.9 us (40%)
  local copies, waits for them, and re-layouts  23.9 us (24%)
  waiting for transfers between devices  15.9 us (16%)
  between operations  14.2 us (14%)
  other arithmetic  5.66 us (6%)
    psum x1, blocking collectives, shards(): first_sum = lax.psum(jnp.take(wall_term, first_rows, axis=0), 'cell')  19.2 us
    unnamed x21, local copies, waits for them, and re-layouts  16 us
    unnamed x4, waiting for transfers between devices  15.9 us
    all_gather x1, blocking collectives, shards(): lag_block = lax.all_gather(lag_density, 'cell', axis=2, tiled=True)  13.4 us
    all_gather x1, blocking collectives, shards(): force_block = lax.all_gather(forces, 'wall', axis=2, tiled=True)  7.22 us
    dynamic_slice x4, local copies, waits for them, and re-layouts, position_at(): lax.dynamic_slice_in_dim(mem_pos, block_index * piece_len, piece_len, 1)  2.75 us
  transfers between devices with their start and end apart: 2, of which 1 were waited for; matrix products, arithmetic and copies ran while one was open for 18% of the time, Pallas kernels for 0%

commit v1 on v0

--- a/solution.py
+++ b/solution.py
@@ -1,8 +1,11 @@
+import functools
 import math
 
 import jax
 import jax.numpy as jnp
 from jax import lax
+from jax.experimental import pallas as pl
+from jax.experimental.pallas import tpu as pltpu
 from jax.sharding import PartitionSpec as P
 
 stokes_coef = 1.0 / (8.0 * math.pi)
@@ -107,6 +110,369 @@
     membrane_velocity = jnp.zeros_like(batched).at[batch_order].set(batched)
     return (membrane_velocity, wall_density)
 
+LANES = 128
+MESH = pl.DeviceIdType.MESH
+NT = (((1,), (1,)), ((), ()))
+
+
+def nearest(position, rank, count):
+    mirrored = position >= (count + 1) // 2
+    here = jnp.where(mirrored, count - 1 - position, position)
+    other = jnp.where(rank <= here, rank - 1, rank)
+    return jnp.where(mirrored, count - 1 - other, other)
+
+
+def fused_kernel(
+    cells,
+    walls,
+    mem_ref,
+    force_ref,
+    wall_ref,
+    normal_ref,
+    data_ref,
+    lag_ref,
+    order_ref,
+    out_ref,
+    density_ref,
+    blocks,
+    mem_all,
+    wall_all,
+    normal_all,
+    first_all,
+    wall_cols,
+    mem_cols,
+    single_all,
+    double_all,
+    block_send,
+    block_recv,
+    forward_send,
+    mem_send,
+    mem_recv,
+    pos_send,
+    pos_recv,
+    first_send,
+    first_recv,
+):
+    cell = lax.axis_index("cell")
+    wall = lax.axis_index("wall")
+    columns = order_ref.shape[1]
+    halfway = columns // 2
+    point_count = mem_ref.shape[1]
+    wall_count = wall_ref.shape[1]
+    own_points = force_ref.shape[2]
+    shard_width = lag_ref.shape[2]
+
+    cell_peers = [lax.rem(cell + step, cells) for step in range(1, cells)]
+    wall_peers = [lax.rem(wall + step, walls) for step in range(1, walls)]
+
+    barrier = pltpu.get_barrier_semaphore()
+    for peer in cell_peers:
+        pl.semaphore_signal(barrier, inc=1, device_id={"cell": peer}, device_id_type=MESH)
+    for peer in wall_peers:
+        pl.semaphore_signal(barrier, inc=1, device_id={"wall": peer}, device_id_type=MESH)
+
+    order_row = order_ref[...]
+    row_ids = lax.broadcasted_iota(jnp.int32, (columns, columns), 0)
+    col_ids = lax.broadcasted_iota(jnp.int32, (columns, columns), 1)
+    scatter = (row_ids == order_row).astype(jnp.float32).astype(jnp.bfloat16)
+    unit = (row_ids == col_ids).astype(jnp.float32).astype(jnp.bfloat16)
+    gather_f32 = lax.dot_general(unit, scatter, NT, preferred_element_type=jnp.float32)
+    gather = gather_f32.astype(jnp.bfloat16)
+
+    for j in range(3):
+        rows = jnp.dot(gather, force_ref[j], preferred_element_type=jnp.float32)
+        packed = jnp.concatenate([rows[:halfway], rows[halfway:]], axis=1)
+        blocks[cell, wall, j] = packed.astype(jnp.bfloat16)
+    lag_rows = [lag_ref[j].astype(jnp.float32) for j in range(3)]
+    room = 2 * own_points - 3 * shard_width
+    lag_rows.append(jnp.zeros((halfway, room), jnp.float32))
+    blocks[cell, wall, 3] = jnp.concatenate(lag_rows, axis=1).astype(jnp.bfloat16)
+    mem_all[cell] = mem_ref[...]
+    wall_all[wall] = wall_ref[...]
+    normal_all[wall] = normal_ref[...]
+
+    def block_copy(source, to_cell, rank):
+        return pltpu.make_async_remote_copy(
+            blocks.at[source, wall],
+            blocks.at[source, wall],
+            block_send.at[rank],
+            block_recv.at[source, wall],
+            device_id={"cell": to_cell},
+            device_id_type=MESH,
+        )
+
+    def forward_copy(source_cell, source_wall, to_wall, rank, slot):
+        return pltpu.make_async_remote_copy(
+            blocks.at[source_cell, source_wall],
+            blocks.at[source_cell, source_wall],
+            forward_send.at[rank, slot],
+            block_recv.at[source_cell, source_wall],
+            device_id={"wall": to_wall},
+            device_id_type=MESH,
+        )
+
+    def mem_copy(source, to_cell, rank):
+        return pltpu.make_async_remote_copy(
+            mem_ref,
+            mem_all.at[source],
+            mem_send.at[rank],
+            mem_recv.at[source],
+            device_id={"cell": to_cell},
+            device_id_type=MESH,
+        )
+
+    def pos_copies(source, to_wall, rank):
+        return [
+            pltpu.make_async_remote_copy(
+                given,
+                held.at[source],
+                pos_send.at[rank, kind],
+                pos_recv.at[source, kind],
+                device_id={"wall": to_wall},
+                device_id_type=MESH,
+            )
+            for kind, (given, held) in enumerate(((wall_ref, wall_all), (normal_ref, normal_all)))
+        ]
+
+    def first_copy(source, to_wall, rank):
+        return pltpu.make_async_remote_copy(
+            first_all.at[source],
+            first_all.at[source],
+            first_send.at[rank],
+            first_recv.at[source],
+            device_id={"wall": to_wall},
+            device_id_type=MESH,
+        )
+
+    pl.semaphore_wait(barrier, cells + walls - 2)
+
+    sent = []
+    for rank in range(cells - 1):
+        sent.append(block_copy(cell, nearest(cell, cells - 1 - rank, cells), rank))
+        sent[-1].start()
+    for rank, peer in enumerate(wall_peers):
+        sent.append(forward_copy(cell, wall, peer, 0, rank))
+        sent[-1].start()
+    for rank, peer in enumerate(cell_peers):
+        sent.append(mem_copy(cell, peer, rank))
+        sent[-1].start()
+    for rank, peer in enumerate(wall_peers):
+        for copy in pos_copies(wall, peer, rank):
+            sent.append(copy)
+            copy.start()
+
+    data_rows = [
+        jnp.dot(gather_f32, data_ref[j], precision=lax.Precision.HIGHEST) for j in range(3)
+    ]
+    for j in range(3):
+        wall_cols[j] = jnp.broadcast_to(wall_ref[j : j + 1, :], (LANES, wall_count)).T
+        mem_cols[j] = jnp.broadcast_to(mem_ref[j : j + 1, :], (LANES, point_count)).T
+
+    def fill_single(source):
+        for start in range(0, point_count, LANES):
+            apart = [
+                wall_cols[j] - mem_all[source, j : j + 1, start : start + LANES] for j in range(3)
+            ]
+            square = apart[0] * apart[0] + apart[1] * apart[1] + apart[2] * apart[2]
+            inverse = lax.rsqrt(square)
+            scaled = stokes_coef * inverse
+            cube = scaled * (inverse * inverse)
+            for j in range(3):
+                along = apart[j] * cube
+                for i in range(j + 1):
+                    element = along * apart[i]
+                    if i == j:
+                        element = element + scaled
+                    element = element.astype(jnp.bfloat16)
+                    for a, b in {(i, j), (j, i)}:
+                        single_all[
+                            source,
+                            a * wall_count : (a + 1) * wall_count,
+                            b * point_count + start : b * point_count + start + LANES,
+                        ] = element
+
+    def fill_double(source):
+        own = pl.ds(pl.multiple_of(wall * own_points, own_points), own_points)
+        for start in range(0, wall_count, LANES):
+            apart = [
+                mem_cols[j, own, :] - wall_all[source, j : j + 1, start : start + LANES]
+                for j in range(3)
+            ]
+            square = apart[0] * apart[0] + apart[1] * apart[1] + apart[2] * apart[2]
+            inverse = lax.rsqrt(square)
+            flux = (
+                apart[0] * normal_all[source, 0:1, start : start + LANES]
+                + apart[1] * normal_all[source, 1:2, start : start + LANES]
+                + apart[2] * normal_all[source, 2:3, start : start + LANES]
+            )
+            inverse_square = inverse * inverse
+            fifth = inverse_square * inverse_square * inverse
+            weight = (-6.0 * stokes_coef) * flux * fifth
+            for j in range(3):
+                along = apart[j] * weight
+                for i in range(j + 1):
+                    element = (along * apart[i]).astype(jnp.bfloat16)
+                    for a, b in {(i, j), (j, i)}:
+                        double_all[
+                            source,
+                            a * own_points : (a + 1) * own_points,
+                            b * wall_count + start : b * wall_count + start + LANES,
+                        ] = element
+
+    fill_single(cell)
+    fill_double(wall)
+
+    for rank in range(1, cells):
+        source = nearest(cell, rank, cells)
+        block_copy(source, source, 0).wait_recv()
+        for slot, peer in enumerate(wall_peers):
+            sent.append(forward_copy(source, wall, peer, rank, slot))
+            sent[-1].start()
+        mem_copy(source, source, 0).wait_recv()
+        fill_single(source)
+        if rank == 1:
+            for peer in wall_peers:
+                for copy in pos_copies(peer, peer, 0):
+                    copy.wait_recv()
+                fill_double(peer)
+
+    velocity = jnp.zeros((columns, 3 * wall_count), jnp.float32)
+    for rank in range(cells):
+        source = cell if rank == 0 else nearest(cell, rank, cells)
+        for peer in wall_peers:
+            forward_copy(source, peer, peer, 0, 0).wait_recv()
+        loaded = []
+        for j in range(3):
+            pieces = [blocks[source, k, j] for k in range(walls)]
+            upper = jnp.concatenate([piece[:, :own_points] for piece in pieces], axis=1)
+            lower = jnp.concatenate([piece[:, own_points:] for piece in pieces], axis=1)
+            loaded.append(jnp.concatenate([upper, lower], axis=0))
+        velocity = velocity + lax.dot_general(
+            jnp.concatenate(loaded, axis=1),
+            single_all[source],
+            NT,
+            preferred_element_type=jnp.float32,
+        )
+
+    density = [
+        2.0 * (data_rows[j] - velocity[:, j * wall_count : (j + 1) * wall_count])
+        for j in range(3)
+    ]
+    for j in range(3):
+        first_all[wall, j] = density[j][:halfway].astype(jnp.bfloat16)
+    for rank, peer in enumerate(wall_peers):
+        sent.append(first_copy(wall, peer, rank))
+        sent[-1].start()
+
+    shift = lax.rem((cells - cell) * shard_width, wall_count)
+    for j in range(3):
+        density_ref[j] = pltpu.roll(density[j][halfway:], shift, 1)[:, :shard_width]
+
+    total = jnp.zeros((columns, 3 * own_points), jnp.float32)
+    for source in range(walls):
+        lag = jnp.concatenate(
+            [
+                blocks[k, source, 3, :, j * shard_width : (j + 1) * shard_width]
+                for j in range(3)
+                for k in range(cells)
+            ],
+            axis=1,
+        )
+        placed = jnp.dot(scatter[:, :halfway], lag, preferred_element_type=jnp.float32)
+        total = total + lax.dot_general(
+            placed.astype(jnp.bfloat16), double_all[source], NT, preferred_element_type=jnp.float32
+        )
+
+    for rank in range(walls):
+        source = wall
+        if rank:
+            source = wall_peers[rank - 1]
+            first_copy(source, source, 0).wait_recv()
+        first = jnp.concatenate([first_all[source, j] for j in range(3)], axis=1)
+        placed = jnp.dot(scatter[:, halfway:], first, preferred_element_type=jnp.float32)
+        total = total + lax.dot_general(
+            placed.astype(jnp.bfloat16), double_all[source], NT, preferred_element_type=jnp.float32
+        )
+    for i in range(3):
+        out_ref[i] = total[:, i * own_points : (i + 1) * own_points]
+
+    for copy in sent:
+        copy.wait_send()
+
+
+def fused_shards(cells, walls, mem_pos, forces, wall_pos, wall_normal, wall_data, lag_density, batch_order):
+    columns = forces.shape[0]
+    halfway = columns // 2
+    point_count = mem_pos.shape[1]
+    wall_count = wall_pos.shape[1]
+    own_points = forces.shape[2]
+    shard_width = lag_density.shape[2]
+    dma = pltpu.SemaphoreType.DMA
+    vmem = pl.BlockSpec(memory_space=pltpu.VMEM)
+    velocity, density = pl.pallas_call(
+        functools.partial(fused_kernel, cells, walls),
+        out_shape=(
+            jax.ShapeDtypeStruct((3, columns, own_points), jnp.float32),
+            jax.ShapeDtypeStruct((3, halfway, shard_width), jnp.float32),
+        ),
+        in_specs=[vmem] * 7,
+        out_specs=(vmem, vmem),
+        scratch_shapes=[
+            pltpu.VMEM((cells, walls, 4, halfway, 2 * own_points), jnp.bfloat16),
+            pltpu.VMEM((cells, 3, point_count), jnp.float32),
+            pltpu.VMEM((walls, 3, wall_count), jnp.float32),
+            pltpu.VMEM((walls, 3, wall_count), jnp.float32),
+            pltpu.VMEM((walls, 3, halfway, wall_count), jnp.bfloat16),
+            pltpu.VMEM((3, wall_count, LANES), jnp.float32),
+            pltpu.VMEM((3, point_count, LANES), jnp.float32),
+            pltpu.VMEM((cells, 3 * wall_count, 3 * point_count), jnp.bfloat16),
+            pltpu.VMEM((walls, 3 * own_points, 3 * wall_count), jnp.bfloat16),
+            dma((cells,)),
+            dma((cells, walls)),
+            dma((cells, walls)),
+            dma((cells,)),
+            dma((cells,)),
+            dma((walls, 2)),
+            dma((walls, 2)),
+            dma((walls,)),
+            dma((walls,)),
+        ],
+        compiler_params=pltpu.CompilerParams(
+            collective_id=0, has_side_effects=True, vmem_limit_bytes=VMEM_GRANT
+        ),
+        name="coupling",
+    )(
+        mem_pos,
+        jnp.transpose(forces, (1, 0, 2)),
+        wall_pos,
+        wall_normal,
+        jnp.transpose(wall_data, (1, 0, 2)),
+        jnp.transpose(lag_density, (1, 0, 2)),
+        batch_order.reshape(1, columns),
+    )
+    return (jnp.transpose(velocity, (1, 0, 2)), jnp.transpose(density, (1, 0, 2)))
+
+
+VMEM_GRANT = 32 * 1024 * 1024
+
+
+def step(cells, walls, mem_pos, forces, wall_pos, *rest):
+    point_count = mem_pos.shape[1]
+    wall_count = wall_pos.shape[1]
+    own_points = forces.shape[2]
+    shard_width = rest[2].shape[2]
+    tiles = 18 * wall_count * (cells * point_count + walls * own_points)
+    fits = tiles <= VMEM_GRANT // 2
+    aligned = (
+        point_count % LANES == 0
+        and wall_count % LANES == 0
+        and 2 * own_points == LANES
+        and 3 * shard_width <= LANES
+    )
+    if fits and aligned:
+        return fused_shards(cells, walls, mem_pos, forces, wall_pos, *rest)
+    return shards(mem_pos, forces, wall_pos, *rest)
+
 
 def solution(mesh):
     placed = (
@@ -119,7 +485,7 @@
         P(),
     )
     return jax.shard_map(
-        shards,
+        functools.partial(step, mesh.shape["cell"], mesh.shape["wall"]),
         mesh=mesh,
         in_specs=placed,
         out_specs=(

time: 101 us -> 21.9 us (0.22)
  blocking collectives: 39.9 us -> 0 us
  local copies, waits for them, and re-layouts: 23.9 us -> 4.83 us
  Pallas kernels: 0 us -> 16.1 us
  waiting for transfers between devices: 15.9 us -> 0 us
  between operations: 14.2 us -> 0.67 us
  other arithmetic: 5.66 us -> 0 us
    all_gather x2 -> x0, blocking collectives: 20.6 us -> none  [the longest x1 13.4 us: shards(): lag_block = lax.all_gather(lag_density, 'cell', axis=2, tiled=True)]
    psum x1 -> x0, blocking collectives: 19.2 us -> none  [shards(): first_sum = lax.psum(jnp.take(wall_term, first_rows, axis=0), 'cell')]
    pallas_call x0 -> x1, Pallas kernels: none -> 16.1 us  [fused_shards(): pl.pallas_call(functools.partial(fused_kernel, cells, walls), out_shape=(...]
    unnamed x4 -> x0, waiting for transfers between devices: 15.9 us -> none
    unnamed x21 -> x16, local copies, waits for them, and re-layouts: 16 us -> 4.83 us
    reduce_sum x4 -> x0, other arithmetic: 3.31 us -> none  [the longest x2 1.71 us: double_tile(): normal_flux = jnp.sum(separation * normals[:, :, None], axis=0)]
    dynamic_slice x6 -> x0, local copies, waits for them, and re-layouts: 2.79 us -> none  [the longest x4 2.75 us: position_at(): lax.dynamic_slice_in_dim(mem_pos, block_index * piece_len, piece_len, 1)]
    gather x4 -> x0, local copies, waits for them, and re-layouts: 2.35 us -> none  [the longest x1 0.59 us: shards(): jnp.take(wall_data, second_rows, axis=0)]
  transfers between devices with their start and end apart: 2 -> 0, of which waited for: 1 -> 0; matrix products, arithmetic and copies ran while one was open for 18% -> 0% of each run, Pallas kernels for 0% -> 0%
where the time goes in v1:
time: 21.9 us; the launch traced here: 21.6 us
  Pallas kernels  16.1 us (74%)
  local copies, waits for them, and re-layouts  4.83 us (22%)
  between operations  0.67 us (3%)
    pallas_call x1, Pallas kernels, fused_shards(): pl.pallas_call(functools.partial(fused_kernel, cells, walls), out_shape=(...  16.1 us
    unnamed x16, local copies, waits for them, and re-layouts  4.83 us

profile of v1, /device:TPU:0, one launch (start us, length us, event | category | flops | bytes accessed | tf_op | source)
XLA Modules:
  0.0 21.6 jit_solution(10805843298256501327)
XLA Ops:
  0.6 0.0 copy-start.3
  0.6 0.0 copy-start.4
  0.7 0.0 copy-start.6
  0.7 0.7 %copy-done.3 = f32[3,256]{1,0:T(4,128)S(1)} copy-done((f32[3,256]{1,0:T(4,128)S(1)}, f32[3,256]{1,0:T(4,128)}, u32[]{:S(2)}) %copy-start.3) | copy-done | bytes 3096
  1.3 0.0 copy-done.4
  1.3 0.0 copy-done.6
  1.3 0.0 copy-start
  1.3 0.8 %copy-done = f32[32,3,128]{2,0,1:T(8,128)S(1)} copy-done((f32[32,3,128]{2,0,1:T(8,128)S(1)}, f32[32,3,128]{2,0,1:T(8,128)}, u32[]{:S(2)}) %copy-start) | copy-done | bytes 49176
  2.1 0.0 copy-start.1
  2.1 0.7 %copy-done.1 = bf16[32,3,64]{2,0,1:T(8,128)(2,1)S(1)} copy-done((bf16[32,3,64]{2,0,1:T(8,128)(2,1)S(1)}, bf16[32,3,64]{2,0,1:T(8,128)(2,1)}, u32[]{:S(2)}) %copy-start.1) | copy-done | bytes 12312
  2.9 0.0 copy-start.2
  2.9 0.7 %copy-done.2 = bf16[16,3,32]{2,0,1:T(8,128)(2,1)S(1)} copy-done((bf16[16,3,32]{2,0,1:T(8,128)(2,1)S(1)}, bf16[16,3,32]{2,0,1:T(8,128)(2,1)}, u32[]{:S(2)}) %copy-start.2) | copy-done | bytes 3096
  3.6 0.0 copy-start.5
  3.6 0.7 %copy-done.5 = f32[3,128]{1,0:T(4,128)S(1)} copy-done((f32[3,128]{1,0:T(4,128)S(1)}, f32[3,128]{1,0:T(4,128)}, u32[]{:S(2)}) %copy-start.5) | copy-done | bytes 1560
  4.3 16.1 %coupling.1 = (f32[3,32,64]{2,1,0:T(8,128)S(1)}, f32[3,16,32]{2,1,0:T(8,128)S(1)}) custom-call(f32[3,256]{1,0:T(4,128)S(1)} %copy-done.3, bf16[3,32,64]{2,1,0:T(8,128)(2,1)S(1)} %bitcast.9, f32[3,128]{1,0:T(4,128)S(1)} %copy-done.4, f32[3,128]{1,0:T(4,128)S(1)} %copy-done.5, f32[3,32,128]{2,1,0:T(8,128)S(1)} %bitcast.6, bf16[3,16,32]{2,1,0:T(8,128)(2,1)S(1)} %bitcast.10, ...), custom_call_target="tpu_custom_call" | custom-call | tf_op jit(solution)/shard_map/coupling/pallas_call | solution.py:412
  20.3 0.6 %copy.11 = f32[32,3,64]{2,0,1:T(8,128)} copy(f32[32,3,64]{2,0,1:T(8,128)S(1)} %bitcast.7) | data formatting | bytes 49152
  21.0 0.6 %copy.12 = f32[16,3,32]{2,0,1:T(8,128)} copy(f32[16,3,32]{2,0,1:T(8,128)S(1)} %bitcast.8) | data formatting | bytes 12288
Async XLA Ops:
  0.6 0.7 %copy-start.3 = (f32[3,256]{1,0:T(4,128)S(1)}, f32[3,256]{1,0:T(4,128)}, u32[]{:S(2)}) copy-start(f32[3,256]{1,0:T(4,128)} %mem_ref.1) | copy-start | bytes 9220
  0.6 0.7 %copy-start.4 = (f32[3,128]{1,0:T(4,128)S(1)}, f32[3,128]{1,0:T(4,128)}, u32[]{:S(2)}) copy-start(f32[3,128]{1,0:T(4,128)} %wall_ref.1) | copy-start | bytes 4612
  0.7 0.7 %copy-start.6 = (s32[32]{0:T(128)S(1)}, s32[32]{0:T(128)}, u32[]{:S(2)}) copy-start(s32[32]{0:T(128)} %param.13) | copy-start | bytes 388
  1.3 0.8 %copy-start = (f32[32,3,128]{2,0,1:T(8,128)S(1)}, f32[32,3,128]{2,0,1:T(8,128)}, u32[]{:S(2)}) copy-start(f32[32,3,128]{2,0,1:T(8,128)} %param.11) | copy-start | bytes 147460
  2.1 0.7 %copy-start.1 = (bf16[32,3,64]{2,0,1:T(8,128)(2,1)S(1)}, bf16[32,3,64]{2,0,1:T(8,128)(2,1)}, u32[]{:S(2)}) copy-start(bf16[32,3,64]{2,0,1:T(8,128)(2,1)} %param.8) | copy-start | bytes 36868
  2.9 0.7 %copy-start.2 = (bf16[16,3,32]{2,0,1:T(8,128)(2,1)S(1)}, bf16[16,3,32]{2,0,1:T(8,128)(2,1)}, u32[]{:S(2)}) copy-start(bf16[16,3,32]{2,0,1:T(8,128)(2,1)} %param.12) | copy-start | bytes 9220
  3.6 0.7 %copy-start.5 = (f32[3,128]{1,0:T(4,128)S(1)}, f32[3,128]{1,0:T(4,128)}, u32[]{:S(2)}) copy-start(f32[3,128]{1,0:T(4,128)} %normal_ref.1) | copy-start | bytes 4612

commit v2 on v1

--- a/solution.py
+++ b/solution.py
@@ -125,15 +125,19 @@
 def fused_kernel(
     cells,
     walls,
-    mem_ref,
+    mem_hbm,
+    force_hbm,
+    wall_hbm,
+    normal_hbm,
+    data_hbm,
+    lag_hbm,
+    order_hbm,
+    out_ref,
+    density_ref,
     force_ref,
-    wall_ref,
-    normal_ref,
     data_ref,
     lag_ref,
     order_ref,
-    out_ref,
-    density_ref,
     blocks,
     mem_all,
     wall_all,
@@ -143,6 +147,7 @@
     mem_cols,
     single_all,
     double_all,
+    load_sem,
     block_send,
     block_recv,
     forward_send,
@@ -157,10 +162,27 @@
     wall = lax.axis_index("wall")
     columns = order_ref.shape[1]
     halfway = columns // 2
-    point_count = mem_ref.shape[1]
-    wall_count = wall_ref.shape[1]
+    point_count = mem_hbm.shape[1]
+    wall_count = wall_hbm.shape[1]
     own_points = force_ref.shape[2]
     shard_width = lag_ref.shape[2]
+
+    loads = [
+        pltpu.make_async_copy(given, held, load_sem.at[at])
+        for at, (given, held) in enumerate(
+            (
+                (order_hbm, order_ref),
+                (force_hbm, force_ref),
+                (lag_hbm, lag_ref),
+                (mem_hbm, mem_all.at[cell]),
+                (wall_hbm, wall_all.at[wall]),
+                (normal_hbm, normal_all.at[wall]),
+                (data_hbm, data_ref),
+            )
+        )
+    ]
+    for load in loads:
+        load.start()
 
     cell_peers = [lax.rem(cell + step, cells) for step in range(1, cells)]
     wall_peers = [lax.rem(wall + step, walls) for step in range(1, walls)]
@@ -171,6 +193,7 @@
     for peer in wall_peers:
         pl.semaphore_signal(barrier, inc=1, device_id={"wall": peer}, device_id_type=MESH)
 
+    loads[0].wait()
     order_row = order_ref[...]
     row_ids = lax.broadcasted_iota(jnp.int32, (columns, columns), 0)
     col_ids = lax.broadcasted_iota(jnp.int32, (columns, columns), 1)
@@ -179,41 +202,48 @@
     gather_f32 = lax.dot_general(unit, scatter, NT, preferred_element_type=jnp.float32)
     gather = gather_f32.astype(jnp.bfloat16)
 
-    for j in range(3):
-        rows = jnp.dot(gather, force_ref[j], preferred_element_type=jnp.float32)
-        packed = jnp.concatenate([rows[:halfway], rows[halfway:]], axis=1)
-        blocks[cell, wall, j] = packed.astype(jnp.bfloat16)
+    loads[1].wait()
+    rows = [jnp.dot(gather, force_ref[j], preferred_element_type=jnp.float32) for j in range(3)]
+    loads[2].wait()
     lag_rows = [lag_ref[j].astype(jnp.float32) for j in range(3)]
-    room = 2 * own_points - 3 * shard_width
-    lag_rows.append(jnp.zeros((halfway, room), jnp.float32))
-    blocks[cell, wall, 3] = jnp.concatenate(lag_rows, axis=1).astype(jnp.bfloat16)
-    mem_all[cell] = mem_ref[...]
-    wall_all[wall] = wall_ref[...]
-    normal_all[wall] = normal_ref[...]
-
-    def block_copy(source, to_cell, rank):
+    spare = jnp.zeros((halfway, own_points - 2 * shard_width), jnp.float32)
+    unused = jnp.zeros((halfway, own_points - shard_width), jnp.float32)
+    halves = (
+        ([row[:halfway] for row in rows], (lag_rows[0], lag_rows[1], spare)),
+        ([row[halfway:] for row in rows], (lag_rows[2], unused)),
+    )
+    for wave, (part, rest) in enumerate(halves):
+        rest = [piece for piece in rest if piece.shape[1]]
+        pair = jnp.concatenate([part[0], part[1]], axis=1)
+        blocks[wave, cell, wall, 0] = pair.astype(jnp.bfloat16)
+        pair = jnp.concatenate([part[2], *rest], axis=1)
+        blocks[wave, cell, wall, 1] = pair.astype(jnp.bfloat16)
+    for load in loads[3:6]:
+        load.wait()
+
+    def block_copy(wave, source, to_cell, rank):
         return pltpu.make_async_remote_copy(
-            blocks.at[source, wall],
-            blocks.at[source, wall],
-            block_send.at[rank],
-            block_recv.at[source, wall],
+            blocks.at[wave, source, wall],
+            blocks.at[wave, source, wall],
+            block_send.at[wave, rank],
+            block_recv.at[wave, source, wall],
             device_id={"cell": to_cell},
             device_id_type=MESH,
         )
 
-    def forward_copy(source_cell, source_wall, to_wall, rank, slot):
+    def forward_copy(wave, source_cell, source_wall, to_wall, rank, slot):
         return pltpu.make_async_remote_copy(
-            blocks.at[source_cell, source_wall],
-            blocks.at[source_cell, source_wall],
-            forward_send.at[rank, slot],
-            block_recv.at[source_cell, source_wall],
+            blocks.at[wave, source_cell, source_wall],
+            blocks.at[wave, source_cell, source_wall],
+            forward_send.at[wave, rank, slot],
+            block_recv.at[wave, source_cell, source_wall],
             device_id={"wall": to_wall},
             device_id_type=MESH,
         )
 
     def mem_copy(source, to_cell, rank):
         return pltpu.make_async_remote_copy(
-            mem_ref,
+            mem_all.at[source],
             mem_all.at[source],
             mem_send.at[rank],
             mem_recv.at[source],
@@ -224,14 +254,14 @@
     def pos_copies(source, to_wall, rank):
         return [
             pltpu.make_async_remote_copy(
-                given,
+                held.at[source],
                 held.at[source],
                 pos_send.at[rank, kind],
                 pos_recv.at[source, kind],
                 device_id={"wall": to_wall},
                 device_id_type=MESH,
             )
-            for kind, (given, held) in enumerate(((wall_ref, wall_all), (normal_ref, normal_all)))
+            for kind, held in enumerate((wall_all, normal_all))
         ]
 
     def first_copy(source, to_wall, rank):
@@ -247,26 +277,35 @@
     pl.semaphore_wait(barrier, cells + walls - 2)
 
     sent = []
-    for rank in range(cells - 1):
-        sent.append(block_copy(cell, nearest(cell, cells - 1 - rank, cells), rank))
-        sent[-1].start()
-    for rank, peer in enumerate(wall_peers):
-        sent.append(forward_copy(cell, wall, peer, 0, rank))
-        sent[-1].start()
+
+    def send(copy):
+        sent.append(copy)
+        copy.start()
+
+    def send_own(wave):
+        for rank in range(cells - 1):
+            send(block_copy(wave, cell, nearest(cell, cells - 1 - rank, cells), rank))
+        for slot, peer in enumerate(wall_peers):
+            send(forward_copy(wave, cell, wall, peer, 0, slot))
+
+    def pass_on(wave, rank):
+        source = nearest(cell, rank, cells)
+        block_copy(wave, source, source, 0).wait_recv()
+        for slot, peer in enumerate(wall_peers):
+            send(forward_copy(wave, source, wall, peer, rank, slot))
+
+    send_own(0)
     for rank, peer in enumerate(cell_peers):
-        sent.append(mem_copy(cell, peer, rank))
-        sent[-1].start()
+        send(mem_copy(cell, peer, rank))
     for rank, peer in enumerate(wall_peers):
         for copy in pos_copies(wall, peer, rank):
-            sent.append(copy)
-            copy.start()
-
-    data_rows = [
-        jnp.dot(gather_f32, data_ref[j], precision=lax.Precision.HIGHEST) for j in range(3)
-    ]
+            send(copy)
+    send_own(1)
+
     for j in range(3):
-        wall_cols[j] = jnp.broadcast_to(wall_ref[j : j + 1, :], (LANES, wall_count)).T
-        mem_cols[j] = jnp.broadcast_to(mem_ref[j : j + 1, :], (LANES, point_count)).T
+        wall_cols[j] = jnp.broadcast_to(wall_all[wall, j : j + 1, :], (LANES, wall_count)).T
+        mem_cols[j] = jnp.broadcast_to(mem_all[cell, j : j + 1, :], (LANES, point_count)).T
+    loads[6].wait()
 
     def fill_single(source):
         for start in range(0, point_count, LANES):
@@ -323,57 +362,62 @@
     fill_double(wall)
 
     for rank in range(1, cells):
+        pass_on(0, rank)
+    for rank in range(1, cells):
         source = nearest(cell, rank, cells)
-        block_copy(source, source, 0).wait_recv()
-        for slot, peer in enumerate(wall_peers):
-            sent.append(forward_copy(source, wall, peer, rank, slot))
-            sent[-1].start()
         mem_copy(source, source, 0).wait_recv()
         fill_single(source)
-        if rank == 1:
+    for rank in range(1, cells):
+        pass_on(1, rank)
+
+    def single_layer(wave):
+        velocity = jnp.zeros((halfway, 3 * wall_count), jnp.float32)
+        for rank in range(cells):
+            source = cell if rank == 0 else nearest(cell, rank, cells)
             for peer in wall_peers:
-                for copy in pos_copies(peer, peer, 0):
-                    copy.wait_recv()
-                fill_double(peer)
-
-    velocity = jnp.zeros((columns, 3 * wall_count), jnp.float32)
-    for rank in range(cells):
-        source = cell if rank == 0 else nearest(cell, rank, cells)
-        for peer in wall_peers:
-            forward_copy(source, peer, peer, 0, 0).wait_recv()
-        loaded = []
-        for j in range(3):
-            pieces = [blocks[source, k, j] for k in range(walls)]
-            upper = jnp.concatenate([piece[:, :own_points] for piece in pieces], axis=1)
-            lower = jnp.concatenate([piece[:, own_points:] for piece in pieces], axis=1)
-            loaded.append(jnp.concatenate([upper, lower], axis=0))
-        velocity = velocity + lax.dot_general(
-            jnp.concatenate(loaded, axis=1),
-            single_all[source],
-            NT,
-            preferred_element_type=jnp.float32,
-        )
-
-    density = [
-        2.0 * (data_rows[j] - velocity[:, j * wall_count : (j + 1) * wall_count])
-        for j in range(3)
+                forward_copy(wave, source, peer, peer, 0, 0).wait_recv()
+            pairs = [blocks[wave, source, k, 0] for k in range(walls)]
+            thirds = [blocks[wave, source, k, 1] for k in range(walls)]
+            loaded = [piece[:, :own_points] for piece in pairs]
+            loaded += [piece[:, own_points:] for piece in pairs]
+            loaded += [piece[:, :own_points] for piece in thirds]
+            velocity = velocity + lax.dot_general(
+                jnp.concatenate(loaded, axis=1),
+                single_all[source],
+                NT,
+                preferred_element_type=jnp.float32,
+            )
+        held = slice(wave * halfway, (wave + 1) * halfway)
+        return [
+            2.0 * (data_rows[j][held] - velocity[:, j * wall_count : (j + 1) * wall_count])
+            for j in range(3)
+        ]
+
+    data_rows = [
+        jnp.dot(gather_f32, data_ref[j], precision=lax.Precision.HIGHEST) for j in range(3)
     ]
+    first_rows = single_layer(0)
     for j in range(3):
-        first_all[wall, j] = density[j][:halfway].astype(jnp.bfloat16)
+        first_all[wall, j] = first_rows[j].astype(jnp.bfloat16)
     for rank, peer in enumerate(wall_peers):
-        sent.append(first_copy(wall, peer, rank))
-        sent[-1].start()
-
+        send(first_copy(wall, peer, rank))
+
+    for peer in wall_peers:
+        for copy in pos_copies(peer, peer, 0):
+            copy.wait_recv()
+        fill_double(peer)
     shift = lax.rem((cells - cell) * shard_width, wall_count)
+    second_rows = single_layer(1)
     for j in range(3):
-        density_ref[j] = pltpu.roll(density[j][halfway:], shift, 1)[:, :shard_width]
-
+        density_ref[j] = pltpu.roll(second_rows[j], shift, 1)[:, :shard_width]
+
+    lag_places = ((0, own_points), (0, own_points + shard_width), (1, own_points))
     total = jnp.zeros((columns, 3 * own_points), jnp.float32)
     for source in range(walls):
         lag = jnp.concatenate(
             [
-                blocks[k, source, 3, :, j * shard_width : (j + 1) * shard_width]
-                for j in range(3)
+                blocks[wave, k, source, 1, :, start : start + shard_width]
+                for wave, start in lag_places
                 for k in range(cells)
             ],
             axis=1,
@@ -400,6 +444,15 @@
         copy.wait_send()
 
 
+def write_kernel(velocity_ref, density_ref, velocity_hbm, density_hbm, sem):
+    first = pltpu.make_async_copy(velocity_ref, velocity_hbm, sem.at[0])
+    second = pltpu.make_async_copy(density_ref, density_hbm, sem.at[1])
+    first.start()
+    second.start()
+    first.wait()
+    second.wait()
+
+
 def fused_shards(cells, walls, mem_pos, forces, wall_pos, wall_normal, wall_data, lag_density, batch_order):
     columns = forces.shape[0]
     halfway = columns // 2
@@ -409,16 +462,21 @@
     shard_width = lag_density.shape[2]
     dma = pltpu.SemaphoreType.DMA
     vmem = pl.BlockSpec(memory_space=pltpu.VMEM)
+    hbm = pl.BlockSpec(memory_space=pltpu.HBM)
     velocity, density = pl.pallas_call(
         functools.partial(fused_kernel, cells, walls),
         out_shape=(
-            jax.ShapeDtypeStruct((3, columns, own_points), jnp.float32),
-            jax.ShapeDtypeStruct((3, halfway, shard_width), jnp.float32),
+            pltpu.VMEM((3, columns, own_points), jnp.float32),
+            pltpu.VMEM((3, halfway, shard_width), jnp.float32),
         ),
-        in_specs=[vmem] * 7,
+        in_specs=[hbm] * 7,
         out_specs=(vmem, vmem),
         scratch_shapes=[
-            pltpu.VMEM((cells, walls, 4, halfway, 2 * own_points), jnp.bfloat16),
+            pltpu.VMEM((3, columns, own_points), jnp.bfloat16),
+            pltpu.VMEM((3, columns, wall_count), jnp.float32),
+            pltpu.VMEM((3, halfway, shard_width), jnp.bfloat16),
+            pltpu.VMEM((1, columns), jnp.int32),
+            pltpu.VMEM((2, cells, walls, 2, halfway, 2 * own_points), jnp.bfloat16),
             pltpu.VMEM((cells, 3, point_count), jnp.float32),
             pltpu.VMEM((walls, 3, wall_count), jnp.float32),
             pltpu.VMEM((walls, 3, wall_count), jnp.float32),
@@ -427,14 +485,15 @@
             pltpu.VMEM((3, point_count, LANES), jnp.float32),
             pltpu.VMEM((cells, 3 * wall_count, 3 * point_count), jnp.bfloat16),
             pltpu.VMEM((walls, 3 * own_points, 3 * wall_count), jnp.bfloat16),
+            dma((7,)),
+            dma((2, cells - 1)),
+            dma((2, cells, walls)),
+            dma((2, cells, walls - 1)),
+            dma((cells - 1,)),
             dma((cells,)),
-            dma((cells, walls)),
-            dma((cells, walls)),
-            dma((cells,)),
-            dma((cells,)),
+            dma((walls - 1, 2)),
             dma((walls, 2)),
-            dma((walls, 2)),
-            dma((walls,)),
+            dma((walls - 1,)),
             dma((walls,)),
         ],
         compiler_params=pltpu.CompilerParams(
@@ -450,10 +509,22 @@
         jnp.transpose(lag_density, (1, 0, 2)),
         batch_order.reshape(1, columns),
     )
+    velocity, density = pl.pallas_call(
+        write_kernel,
+        out_shape=(
+            jax.ShapeDtypeStruct(velocity.shape, velocity.dtype),
+            jax.ShapeDtypeStruct(density.shape, density.dtype),
+        ),
+        in_specs=[vmem] * 2,
+        out_specs=(hbm, hbm),
+        scratch_shapes=[dma((2,))],
+        compiler_params=pltpu.CompilerParams(vmem_limit_bytes=1024 * 1024),
+        name="write",
+    )(velocity, density)
     return (jnp.transpose(velocity, (1, 0, 2)), jnp.transpose(density, (1, 0, 2)))
 
 
-VMEM_GRANT = 32 * 1024 * 1024
+VMEM_GRANT = 60 * 1024 * 1024
 
 
 def step(cells, walls, mem_pos, forces, wall_pos, *rest):
@@ -467,7 +538,7 @@
         point_count % LANES == 0
         and wall_count % LANES == 0
         and 2 * own_points == LANES
-        and 3 * shard_width <= LANES
+        and 2 * shard_width <= own_points
     )
     if fits and aligned:
         return fused_shards(cells, walls, mem_pos, forces, wall_pos, *rest)

time: 21.9 us -> 16.9 us (0.77)
  local copies, waits for them, and re-layouts: 4.83 us -> 0 us
    unnamed x16 -> x0, local copies, waits for them, and re-layouts: 4.83 us -> none
    pallas_call x0 -> x1, Pallas kernels: none -> 0.64 us  [fused_shards(): pl.pallas_call(write_kernel, out_shape=(jax.ShapeDtypeStruct(velocity.sha...]
    pallas_call x1, Pallas kernels: 16.1 us -> 15.5 us  [fused_shards(): pl.pallas_call(functools.partial(fused_kernel, cells, walls), out_shape=(...]
where the time goes in v2:
time: 16.9 us; the launch traced here: 16.8 us
  Pallas kernels  16.1 us (95%)
  between operations  0.64 us (4%)
    pallas_call x1, Pallas kernels, fused_shards(): pl.pallas_call(functools.partial(fused_kernel, cells, walls), out_shape=(...  15.5 us
    pallas_call x1, Pallas kernels, fused_shards(): pl.pallas_call(write_kernel, out_shape=(jax.ShapeDtypeStruct(velocity.sha...  0.64 us

profile of v2, /device:TPU:0, one launch (start us, length us, event | category | flops | bytes accessed | tf_op | source)
XLA Modules:
  0.0 16.8 jit_solution(8960705703372039968)
XLA Ops:
  0.6 15.5 %coupling.1 = (f32[3,32,64]{2,1,0:T(8,128)S(1)}, f32[3,16,32]{2,1,0:T(8,128)S(1)}) custom-call(f32[3,256]{1,0:T(4,128)} %mem_hbm.1, bf16[3,32,64]{2,1,0:T(8,128)(2,1)} %bitcast.7, f32[3,128]{1,0:T(4,128)} %wall_hbm.1, f32[3,128]{1,0:T(4,128)} %normal_hbm.1, f32[3,32,128]{2,1,0:T(8,128)} %bitcast.6, bf16[3,16,32]{2,1,0:T(8,128)(2,1)} %bitcast.8, s32[1,32]{1,0:T(1,128)} %bitcast.9), custom_call_target="tpu_custom_call" | custom-call | tf_op jit(solution)/shard_map/coupling/pallas_call | solution.py:466
  16.1 0.6 %write.1 = (f32[3,32,64]{2,1,0:T(8,128)}, f32[3,16,32]{2,1,0:T(8,128)}) custom-call(f32[3,32,64]{2,1,0:T(8,128)S(1)} %get-tuple-element.6.velocity_ref, f32[3,16,32]{2,1,0:T(8,128)S(1)} %get-tuple-element.7.density_ref), custom_call_target="tpu_custom_call" | custom-call | tf_op jit(solution)/shard_map/write/pallas_call | solution.py:512

commit v3 on v2

--- a/solution.py
+++ b/solution.py
@@ -141,7 +141,6 @@
     blocks,
     mem_all,
     wall_all,
-    normal_all,
     first_all,
     wall_cols,
     mem_cols,
@@ -175,8 +174,8 @@
                 (force_hbm, force_ref),
                 (lag_hbm, lag_ref),
                 (mem_hbm, mem_all.at[cell]),
-                (wall_hbm, wall_all.at[wall]),
-                (normal_hbm, normal_all.at[wall]),
+                (wall_hbm, wall_all.at[wall, 0]),
+                (normal_hbm, wall_all.at[wall, 1]),
                 (data_hbm, data_ref),
             )
         )
@@ -251,18 +250,15 @@
             device_id_type=MESH,
         )
 
-    def pos_copies(source, to_wall, rank):
-        return [
-            pltpu.make_async_remote_copy(
-                held.at[source],
-                held.at[source],
-                pos_send.at[rank, kind],
-                pos_recv.at[source, kind],
-                device_id={"wall": to_wall},
-                device_id_type=MESH,
-            )
-            for kind, held in enumerate((wall_all, normal_all))
-        ]
+    def pos_copy(source, to_wall, rank):
+        return pltpu.make_async_remote_copy(
+            wall_all.at[source],
+            wall_all.at[source],
+            pos_send.at[rank],
+            pos_recv.at[source],
+            device_id={"wall": to_wall},
+            device_id_type=MESH,
+        )
 
     def first_copy(source, to_wall, rank):
         return pltpu.make_async_remote_copy(
@@ -298,12 +294,11 @@
     for rank, peer in enumerate(cell_peers):
         send(mem_copy(cell, peer, rank))
     for rank, peer in enumerate(wall_peers):
-        for copy in pos_copies(wall, peer, rank):
-            send(copy)
+        send(pos_copy(wall, peer, rank))
     send_own(1)
 
     for j in range(3):
-        wall_cols[j] = jnp.broadcast_to(wall_all[wall, j : j + 1, :], (LANES, wall_count)).T
+        wall_cols[j] = jnp.broadcast_to(wall_all[wall, 0, j : j + 1, :], (LANES, wall_count)).T
         mem_cols[j] = jnp.broadcast_to(mem_all[cell, j : j + 1, :], (LANES, point_count)).T
     loads[6].wait()
 
@@ -334,15 +329,15 @@
         own = pl.ds(pl.multiple_of(wall * own_points, own_points), own_points)
         for start in range(0, wall_count, LANES):
             apart = [
-                mem_cols[j, own, :] - wall_all[source, j : j + 1, start : start + LANES]
+                mem_cols[j, own, :] - wall_all[source, 0, j : j + 1, start : start + LANES]
                 for j in range(3)
             ]
             square = apart[0] * apart[0] + apart[1] * apart[1] + apart[2] * apart[2]
             inverse = lax.rsqrt(square)
             flux = (
-                apart[0] * normal_all[source, 0:1, start : start + LANES]
-                + apart[1] * normal_all[source, 1:2, start : start + LANES]
-                + apart[2] * normal_all[source, 2:3, start : start + LANES]
+                apart[0] * wall_all[source, 1, 0:1, start : start + LANES]
+                + apart[1] * wall_all[source, 1, 1:2, start : start + LANES]
+                + apart[2] * wall_all[source, 1, 2:3, start : start + LANES]
             )
             inverse_square = inverse * inverse
             fifth = inverse_square * inverse_square * inverse
@@ -360,13 +355,19 @@
 
     fill_single(cell)
     fill_double(wall)
+    data_rows = [
+        jnp.dot(gather_f32, data_ref[j], precision=lax.Precision.HIGHEST) for j in range(3)
+    ]
 
     for rank in range(1, cells):
         pass_on(0, rank)
-    for rank in range(1, cells):
         source = nearest(cell, rank, cells)
         mem_copy(source, source, 0).wait_recv()
         fill_single(source)
+        if rank == 1:
+            for peer in wall_peers:
+                pos_copy(peer, peer, 0).wait_recv()
+                fill_double(peer)
     for rank in range(1, cells):
         pass_on(1, rank)
 
@@ -393,19 +394,12 @@
             for j in range(3)
         ]
 
-    data_rows = [
-        jnp.dot(gather_f32, data_ref[j], precision=lax.Precision.HIGHEST) for j in range(3)
-    ]
     first_rows = single_layer(0)
     for j in range(3):
         first_all[wall, j] = first_rows[j].astype(jnp.bfloat16)
     for rank, peer in enumerate(wall_peers):
         send(first_copy(wall, peer, rank))
 
-    for peer in wall_peers:
-        for copy in pos_copies(peer, peer, 0):
-            copy.wait_recv()
-        fill_double(peer)
     shift = lax.rem((cells - cell) * shard_width, wall_count)
     second_rows = single_layer(1)
     for j in range(3):
@@ -427,6 +421,10 @@
             placed.astype(jnp.bfloat16), double_all[source], NT, preferred_element_type=jnp.float32
         )
 
+    last = len(sent) - (walls - 1)
+    for copy in sent[:last]:
+        copy.wait_send()
+
     for rank in range(walls):
         source = wall
         if rank:
@@ -440,7 +438,7 @@
     for i in range(3):
         out_ref[i] = total[:, i * own_points : (i + 1) * own_points]
 
-    for copy in sent:
+    for copy in sent[last:]:
         copy.wait_send()
 
 
@@ -478,8 +476,7 @@
             pltpu.VMEM((1, columns), jnp.int32),
             pltpu.VMEM((2, cells, walls, 2, halfway, 2 * own_points), jnp.bfloat16),
             pltpu.VMEM((cells, 3, point_count), jnp.float32),
-            pltpu.VMEM((walls, 3, wall_count), jnp.float32),
-            pltpu.VMEM((walls, 3, wall_count), jnp.float32),
+            pltpu.VMEM((walls, 2, 3, wall_count), jnp.float32),
             pltpu.VMEM((walls, 3, halfway, wall_count), jnp.bfloat16),
             pltpu.VMEM((3, wall_count, LANES), jnp.float32),
             pltpu.VMEM((3, point_count, LANES), jnp.float32),
@@ -491,8 +488,8 @@
             dma((2, cells, walls - 1)),
             dma((cells - 1,)),
             dma((cells,)),
-            dma((walls - 1, 2)),
-            dma((walls, 2)),
+            dma((walls - 1,)),
+            dma((walls,)),
             dma((walls - 1,)),
             dma((walls,)),
         ],

time: 16.9 us -> 17.3 us (1.024)
  Pallas kernels: 16.1 us -> 16.5 us
    pallas_call x1, Pallas kernels: 15.5 us -> 15.9 us  [fused_shards(): pl.pallas_call(functools.partial(fused_kernel, cells, walls), out_shape=(...]
where the time goes in v3:
time: 17.3 us; the launch traced here: 17.2 us
  Pallas kernels  16.5 us (95%)
  between operations  0.64 us (4%)
    pallas_call x1, Pallas kernels, fused_shards(): pl.pallas_call(functools.partial(fused_kernel, cells, walls), out_shape=(...  15.9 us
    pallas_call x1, Pallas kernels, fused_shards(): pl.pallas_call(write_kernel, out_shape=(jax.ShapeDtypeStruct(velocity.sha...  0.64 us

profile of v3, /device:TPU:0, one launch (start us, length us, event | category | flops | bytes accessed | tf_op | source)
XLA Modules:
  0.0 17.2 jit_solution(4817049081525453953)
XLA Ops:
  0.6 15.9 %coupling.1 = (f32[3,32,64]{2,1,0:T(8,128)S(1)}, f32[3,16,32]{2,1,0:T(8,128)S(1)}) custom-call(f32[3,256]{1,0:T(4,128)} %mem_hbm.1, bf16[3,32,64]{2,1,0:T(8,128)(2,1)} %bitcast.7, f32[3,128]{1,0:T(4,128)} %wall_hbm.1, f32[3,128]{1,0:T(4,128)} %normal_hbm.1, f32[3,32,128]{2,1,0:T(8,128)} %bitcast.6, bf16[3,16,32]{2,1,0:T(8,128)(2,1)} %bitcast.8, s32[1,32]{1,0:T(1,128)} %bitcast.9), custom_call_target="tpu_custom_call" | custom-call | tf_op jit(solution)/shard_map/coupling/pallas_call | solution.py:464
  16.5 0.6 %write.1 = (f32[3,32,64]{2,1,0:T(8,128)}, f32[3,16,32]{2,1,0:T(8,128)}) custom-call(f32[3,32,64]{2,1,0:T(8,128)S(1)} %get-tuple-element.6.velocity_ref, f32[3,16,32]{2,1,0:T(8,128)S(1)} %get-tuple-element.7.density_ref), custom_call_target="tpu_custom_call" | custom-call | tf_op jit(solution)/shard_map/write/pallas_call | solution.py:509

commit v4 on v3

--- a/solution.py
+++ b/solution.py
@@ -361,13 +361,10 @@
 
     for rank in range(1, cells):
         pass_on(0, rank)
+    for rank in range(1, cells):
         source = nearest(cell, rank, cells)
         mem_copy(source, source, 0).wait_recv()
         fill_single(source)
-        if rank == 1:
-            for peer in wall_peers:
-                pos_copy(peer, peer, 0).wait_recv()
-                fill_double(peer)
     for rank in range(1, cells):
         pass_on(1, rank)
 
@@ -400,6 +397,9 @@
     for rank, peer in enumerate(wall_peers):
         send(first_copy(wall, peer, rank))
 
+    for peer in wall_peers:
+        pos_copy(peer, peer, 0).wait_recv()
+        fill_double(peer)
     shift = lax.rem((cells - cell) * shard_width, wall_count)
     second_rows = single_layer(1)
     for j in range(3):

time: 17.3 us -> 16.8 us (0.971)
  Pallas kernels: 16.5 us -> 16 us
    pallas_call x1, Pallas kernels: 15.9 us -> 15.4 us  [fused_shards(): pl.pallas_call(functools.partial(fused_kernel, cells, walls), out_shape=(...]
where the time goes in v4:
time: 16.8 us; the launch traced here: 16.6 us
  Pallas kernels  16 us (95%)
  between operations  0.64 us (4%)
    pallas_call x1, Pallas kernels, fused_shards(): pl.pallas_call(functools.partial(fused_kernel, cells, walls), out_shape=(...  15.4 us
    pallas_call x1, Pallas kernels, fused_shards(): pl.pallas_call(write_kernel, out_shape=(jax.ShapeDtypeStruct(velocity.sha...  0.64 us

profile of v4, /device:TPU:0, one launch (start us, length us, event | category | flops | bytes accessed | tf_op | source)
XLA Modules:
  0.0 16.6 jit_solution(854244761908114184)
XLA Ops:
  0.6 15.4 %coupling.1 = (f32[3,32,64]{2,1,0:T(8,128)S(1)}, f32[3,16,32]{2,1,0:T(8,128)S(1)}) custom-call(f32[3,256]{1,0:T(4,128)} %mem_hbm.1, bf16[3,32,64]{2,1,0:T(8,128)(2,1)} %bitcast.7, f32[3,128]{1,0:T(4,128)} %wall_hbm.1, f32[3,128]{1,0:T(4,128)} %normal_hbm.1, f32[3,32,128]{2,1,0:T(8,128)} %bitcast.6, bf16[3,16,32]{2,1,0:T(8,128)(2,1)} %bitcast.8, s32[1,32]{1,0:T(1,128)} %bitcast.9), custom_call_target="tpu_custom_call" | custom-call | tf_op jit(solution)/shard_map/coupling/pallas_call | solution.py:464
  16.0 0.6 %write.1 = (f32[3,32,64]{2,1,0:T(8,128)}, f32[3,16,32]{2,1,0:T(8,128)}) custom-call(f32[3,32,64]{2,1,0:T(8,128)S(1)} %get-tuple-element.6.velocity_ref, f32[3,16,32]{2,1,0:T(8,128)S(1)} %get-tuple-element.7.density_ref), custom_call_target="tpu_custom_call" | custom-call | tf_op jit(solution)/shard_map/write/pallas_call | solution.py:509
